TPU v7x, 128 devices: a whole 4x4x4 slice. The times are simulated.
128 devices in a mesh: pipe: 2 (over core), dp: 4 (over x), tensor: 16 (over z, y).
Axes of the slice: x: 4, y: 4, z: 4, core: 2. Of those that a mesh axis runs over, the one named last changes fastest.
Arguments:
- embedded: bfloat16 [512, 4096], P('dp', 'pipe'), may hold values from -6 to 6
- rotation_scaled: float32 [4096, 4096], P(('pipe', 'dp'), 'tensor'), as said below
- value_proj: bfloat16 [2, 4096, 1024], P('pipe', 'tensor'), may hold values from -0.09375 to 0.09375
- output_proj: bfloat16 [2, 1024, 4096], P('pipe', None, 'tensor'), may hold values from -0.1875 to 0.1875
- mid_exponent: int32 [2, 1024], P('pipe'), may hold values from -3 to -1
- cotangent: bfloat16 [512, 4096], P('dp', 'tensor'), may hold values from -6 to 6
Outputs:
- rotation_next: float32 [4096, 4096], P(('pipe', 'dp'), 'tensor')
Inputs may be any that keep to these rules, and one draw needn't show every extreme that they name: rotation_scaled / sqrt(4096) is orthogonal.
All inputs are finite; a program needn't handle non-finite values.
Results may differ from a plain program's by a relative error of at most 0.017.
Values may be sent and summed in bfloat16 or wider, within the bound.
A program may use at most 64 MiB of HBM per device.

v0:
```python
import math
import jax
import jax.numpy as jnp
from jax import lax
from jax.sharding import PartitionSpec as P

D = 4096
MB = 4
TOK_MB = 32


def from_behind(shard, axis, by):
    length = lax.axis_size(axis)
    pairs = [(i, i + by) for i in range(length) if 0 <= i + by < length]
    return lax.ppermute(shard, axis, pairs)


def spread(shard, axis, root):
    mine = lax.axis_index(axis) == root
    return lax.psum(jnp.where(mine, shard, jnp.zeros_like(shard)), axis)


def local(embedded, rotation_scaled, value_proj, output_proj, mid_exponent, cotangent):
    sections = lax.axis_size("pipe")
    section_index = lax.axis_index("pipe")
    column_count = cotangent.shape[1]
    group_rows = embedded.shape[0]
    branch_units = value_proj.shape[2]
    rotation = rotation_scaled / math.sqrt(D)
    rot_rows = lax.all_gather(rotation.astype(jnp.bfloat16), "dp", axis=0, tiled=True)
    embed_part = jnp.dot(embedded, rot_rows, preferred_element_type=jnp.float32)
    start_field = lax.psum(embed_part.astype(jnp.bfloat16), "pipe").astype(jnp.float32)
    start_blocks = start_field.astype(jnp.bfloat16).reshape(MB, TOK_MB, column_count)
    target_blocks = cotangent.reshape(MB, TOK_MB, column_count)
    weight_in = value_proj[0]
    weight_out = output_proj[0]
    bounds = jnp.exp2(mid_exponent[0].astype(jnp.float32))
    lowest = -8.0 * bounds
    highest = 7.0 * bounds
    tick_total = MB + sections - 1

    def forward_tick(tick_count, loop_state):
        received, stash_h, stash_y, stash_r = loop_state
        micro_batch = tick_count - section_index
        active = (micro_batch >= 0) & (micro_batch < MB)
        position = jnp.clip(micro_batch, 0, MB - 1)
        first_input = lax.dynamic_index_in_dim(start_blocks, position, 0, keepdims=False)
        hidden = jnp.where(section_index == 0, first_input, received)
        hidden_f = hidden.astype(jnp.float32)
        partial_value = jnp.dot(hidden, weight_in, preferred_element_type=jnp.float32)
        squares = jnp.sum(hidden_f * hidden_f, axis=1)
        summed, square_total = lax.psum((partial_value, squares), "tensor")
        inv_rms = lax.rsqrt(square_total / D + 1e-05)[:, None]
        clipped = jnp.clip(inv_rms * summed, lowest, highest).astype(jnp.bfloat16)
        branch_out = jnp.dot(clipped, weight_out, preferred_element_type=jnp.float32)
        result = (hidden_f + branch_out).astype(jnp.bfloat16)
        stash_h = jnp.where(
            active, lax.dynamic_update_index_in_dim(stash_h, hidden, position, 0), stash_h
        )
        stash_y = jnp.where(
            active, lax.dynamic_update_index_in_dim(stash_y, summed, position, 0), stash_y
        )
        stash_r = jnp.where(
            active, lax.dynamic_update_index_in_dim(stash_r, inv_rms, position, 0), stash_r
        )
        received = from_behind(result, "pipe", 1)
        return (received, stash_h, stash_y, stash_r)

    forward_state = (
        jnp.zeros((TOK_MB, column_count), jnp.bfloat16),
        jnp.zeros((MB, TOK_MB, column_count), jnp.bfloat16),
        jnp.zeros((MB, TOK_MB, branch_units), jnp.float32),
        jnp.ones((MB, TOK_MB, 1), jnp.float32),
    )
    forward_state = lax.fori_loop(0, tick_total, forward_tick, forward_state)
    saved_h, saved_y, saved_r = (forward_state[1], forward_state[2], forward_state[3])

    def backward_tick(tick_count, loop_state):
        received, stash_g = loop_state
        micro_batch = tick_count - (sections - 1 - section_index)
        active = (micro_batch >= 0) & (micro_batch < MB)
        position = jnp.clip(micro_batch, 0, MB - 1)
        target = lax.dynamic_index_in_dim(target_blocks, position, 0, keepdims=False)
        incoming = jnp.where(section_index == sections - 1, target, received)
        hidden = lax.dynamic_index_in_dim(saved_h, position, 0, keepdims=False)
        summed = lax.dynamic_index_in_dim(saved_y, position, 0, keepdims=False)
        inv_rms = lax.dynamic_index_in_dim(saved_r, position, 0, keepdims=False)
        back_part = lax.dot_general(
            incoming, weight_out, (((1,), (1,)), ((), ())), preferred_element_type=jnp.float32
        )
        back_total = lax.psum(back_part, "tensor")
        gated_rows = inv_rms * summed
        inside = (gated_rows >= lowest) & (gated_rows <= highest)
        scaled_grad = (inv_rms * jnp.where(inside, back_total, 0.0)).astype(jnp.bfloat16)
        linear = lax.dot_general(
            scaled_grad, weight_in, (((1,), (1,)), ((), ())), preferred_element_type=jnp.float32
        )
        statistic = jnp.sum(scaled_grad.astype(jnp.float32) * summed, axis=1, keepdims=True)
        grad_field = (
            incoming.astype(jnp.float32)
            + linear
            - inv_rms * inv_rms / D * statistic * hidden.astype(jnp.float32)
        )
        sent_grad = grad_field.astype(jnp.bfloat16)
        stash_g = jnp.where(
            active & (section_index == 0),
            lax.dynamic_update_index_in_dim(stash_g, sent_grad, position, 0),
            stash_g,
        )
        received = from_behind(sent_grad, "pipe", -1)
        return (received, stash_g)

    backward_state = (
        jnp.zeros((TOK_MB, column_count), jnp.bfloat16),
        jnp.zeros((MB, TOK_MB, column_count), jnp.bfloat16),
    )
    backward_state = lax.fori_loop(0, tick_total, backward_tick, backward_state)
    grad_local = backward_state[1].reshape(group_rows, column_count)
    grad_all = spread(grad_local, "pipe", 0)
    value_part = lax.dot_general(
        grad_all, rot_rows, (((1,), (1,)), ((), ())), preferred_element_type=jnp.float32
    )
    embed_grad = lax.psum(value_part.astype(jnp.bfloat16), "tensor")
    back_part = jnp.dot(embed_grad, rot_rows, preferred_element_type=jnp.float32)
    turned = lax.psum(back_part.astype(jnp.bfloat16), "pipe").astype(jnp.float32)
    first_dirs = (2.0 * jnp.concatenate([turned, -start_field], axis=0)).astype(jnp.bfloat16)
    left_rows = jnp.concatenate([embedded, embed_grad], axis=0)
    right_rows = jnp.concatenate([embed_grad, -embedded], axis=0)
    partial_value = left_rows
    step_one = lax.psum_scatter(
        lax.dot_general(
            partial_value, first_dirs, (((0,), (0,)), ((), ())), preferred_element_type=jnp.float32
        ),
        "dp",
        scatter_dimension=0,
        tiled=True,
    )
    norm_total = lax.psum(jnp.sum(step_one * step_one), ("pipe", "dp", "tensor"))
    step_rate = jnp.sqrt(D / (norm_total + 1e-06))
    first_iter = rotation - 0.5 * step_rate * step_one
    iterate = (rotation + first_iter).astype(jnp.bfloat16)
    iter_rows = lax.all_gather(iterate, "dp", axis=0, tiled=True)
    second_part = jnp.dot(right_rows, iter_rows, preferred_element_type=jnp.float32)
    second_dirs = lax.psum(second_part.astype(jnp.bfloat16), "pipe")
    partial_value = left_rows
    step_two = lax.psum_scatter(
        lax.dot_general(
            partial_value, second_dirs, (((0,), (0,)), ((), ())), preferred_element_type=jnp.float32
        ),
        "dp",
        scatter_dimension=0,
        tiled=True,
    )
    return math.sqrt(D) * (rotation - 0.5 * step_rate * step_two)


def solution(mesh):
    return jax.shard_map(
        local,
        mesh=mesh,
        in_specs=(
            P("dp", "pipe"),
            P(("pipe", "dp"), "tensor"),
            P("pipe", "tensor", None),
            P("pipe", None, "tensor"),
            P("pipe", None),
            P("dp", "tensor"),
        ),
        out_specs=P(("pipe", "dp"), "tensor"),
        check_vma=False,
    )
```

profile of v0, /device:TPU:1, one launch (start us, length us, event | category | flops | bytes accessed | tf_op | source)
XLA Modules:
  0.0 1303.0 jit_solution(10443372473404619989)
XLA Ops:
  8.5 25.7 %all-gather.3.cloned.1.call-done = bf16[2048,256]{1,0:T(8,128)(2,1)} async-done(((bf16[512,256]{1,0:T(8,128)(2,1)}), bf16[2048,256]{1,0:T(8,128)(2,1)}) %all-gather.3.cloned.1.call-update) | async-done | bytes 1048592 | tf_op jit(solution)/shard_map/all_gather | solution.py:30
  36.8 26.2 %all-reduce.8.cloned.1.call-done = bf16[128,256]{0,1:T(8,128)(2,1)} async-done(((bf16[128,256]{0,1:T(8,128)(2,1)}), bf16[128,256]{0,1:T(8,128)(2,1)}) %all-reduce.8.cloned.1.call-update) | async-done | bytes 65552 | tf_op jit(solution)/shard_map/psum | solution.py:32
  64.1 450.8 %while.37 = (s32[]{:T(128)}, bf16[32,256]{1,0:T(8,128)(2,1)S(1)}, bf16[4,32,256]{2,1,0:T(8,128)(2,1)S(1)}, f32[4,32,1024]{2,1,0:T(8,128)S(1)}, f32[4,32,1]{1,2,0...) while((s32[]{:T(128)}, bf16[32,256]{1,0:T(8,128)(2,1)S(1)}, ...), condition=%wide.region_5.6_spmd, body=%wide.region_1.5_spmd.sunk | while | flops 33882280 | bytes 2710062 | solution.py:75
  65.2 33.6 %psum.89 = f32[32]{0:T(128)S(1)} all-reduce(f32[32]{0:T(128)S(1)} %fusion.65), channel_id=1, replica_groups=mesh['pipe'=2,'dp'=4,'tensor'=16] {'tensor'}, use_global_device_ids=true, to_apply=%region_3.3 | all-reduce | flops 32 | bytes 256 | tf_op jit(solution)/shard_map/while/body/eval_jaxpr/psum | solution.py:52
  98.8 51.7 %all-reduce.18.cloned.1.call-done = f32[32,1024]{1,0:T(8,128)} async-done(((f32[32,1024]{1,0:T(8,128)}), f32[32,1024]{1,0:T(8,128)}) %all-reduce.18.cloned.1.call-update) | async-done | bytes 131088 | tf_op jit(solution)/shard_map/while/body/eval_jaxpr/psum | solution.py:52
  157.1 30.9 %psum.89 = f32[32]{0:T(128)S(1)} all-reduce(f32[32]{0:T(128)S(1)} %fusion.65), channel_id=1, replica_groups=mesh['pipe'=2,'dp'=4,'tensor'=16] {'tensor'}, use_global_device_ids=true, to_apply=%region_3.3 | all-reduce | flops 32 | bytes 256 | tf_op jit(solution)/shard_map/while/body/eval_jaxpr/psum | solution.py:52
  188.0 52.1 %all-reduce.18.cloned.1.call-done = f32[32,1024]{1,0:T(8,128)} async-done(((f32[32,1024]{1,0:T(8,128)}), f32[32,1024]{1,0:T(8,128)}) %all-reduce.18.cloned.1.call-update) | async-done | bytes 131088 | tf_op jit(solution)/shard_map/while/body/eval_jaxpr/psum | solution.py:52
  246.7 30.9 %psum.89 = f32[32]{0:T(128)S(1)} all-reduce(f32[32]{0:T(128)S(1)} %fusion.65), channel_id=1, replica_groups=mesh['pipe'=2,'dp'=4,'tensor'=16] {'tensor'}, use_global_device_ids=true, to_apply=%region_3.3 | all-reduce | flops 32 | bytes 256 | tf_op jit(solution)/shard_map/while/body/eval_jaxpr/psum | solution.py:52
  277.6 52.1 %all-reduce.18.cloned.1.call-done = f32[32,1024]{1,0:T(8,128)} async-done(((f32[32,1024]{1,0:T(8,128)}), f32[32,1024]{1,0:T(8,128)}) %all-reduce.18.cloned.1.call-update) | async-done | bytes 131088 | tf_op jit(solution)/shard_map/while/body/eval_jaxpr/psum | solution.py:52
  336.3 30.9 %psum.89 = f32[32]{0:T(128)S(1)} all-reduce(f32[32]{0:T(128)S(1)} %fusion.65), channel_id=1, replica_groups=mesh['pipe'=2,'dp'=4,'tensor'=16] {'tensor'}, use_global_device_ids=true, to_apply=%region_3.3 | all-reduce | flops 32 | bytes 256 | tf_op jit(solution)/shard_map/while/body/eval_jaxpr/psum | solution.py:52
  367.2 52.1 %all-reduce.18.cloned.1.call-done = f32[32,1024]{1,0:T(8,128)} async-done(((f32[32,1024]{1,0:T(8,128)}), f32[32,1024]{1,0:T(8,128)}) %all-reduce.18.cloned.1.call-update) | async-done | bytes 131088 | tf_op jit(solution)/shard_map/while/body/eval_jaxpr/psum | solution.py:52
  426.0 30.9 %psum.89 = f32[32]{0:T(128)S(1)} all-reduce(f32[32]{0:T(128)S(1)} %fusion.65), channel_id=1, replica_groups=mesh['pipe'=2,'dp'=4,'tensor'=16] {'tensor'}, use_global_device_ids=true, to_apply=%region_3.3 | all-reduce | flops 32 | bytes 256 | tf_op jit(solution)/shard_map/while/body/eval_jaxpr/psum | solution.py:52
  456.9 52.4 %all-reduce.18.cloned.1.call-done = f32[32,1024]{1,0:T(8,128)} async-done(((f32[32,1024]{1,0:T(8,128)}), f32[32,1024]{1,0:T(8,128)}) %all-reduce.18.cloned.1.call-update) | async-done | bytes 131088 | tf_op jit(solution)/shard_map/while/body/eval_jaxpr/psum | solution.py:52
  514.9 454.3 %while.38 = (s32[]{:T(128)}, bf16[32,256]{1,0:T(8,128)(2,1)S(1)}, bf16[4,32,256]{2,1,0:T(8,128)(2,1)S(1)}, pred[]{:T(512)}, s32[]{:T(128)}, /*index=5*/bf16[4,32...) while((s32[]{:T(128)}, bf16[32,256]{1,0:T(8,128)(2,1)S(1)}, ...), condition=%wide.region_9.10_spmd, body=%wide.region_6.9_spmd.sunk | while | flops 33988680 | bytes 2565832 | solution.py:117
  515.9 83.2 %all-reduce.20.cloned.1.call-done = f32[32,1024]{1,0:T(8,128)} async-done(((f32[32,1024]{1,0:T(8,128)}), f32[32,1024]{1,0:T(8,128)}) %all-reduce.20.cloned.1.call-update) | async-done | bytes 131088 | tf_op jit(solution)/shard_map/while/body/eval_jaxpr/psum | solution.py:91
  606.8 83.3 %all-reduce.20.cloned.1.call-done = f32[32,1024]{1,0:T(8,128)} async-done(((f32[32,1024]{1,0:T(8,128)}), f32[32,1024]{1,0:T(8,128)}) %all-reduce.20.cloned.1.call-update) | async-done | bytes 131088 | tf_op jit(solution)/shard_map/while/body/eval_jaxpr/psum | solution.py:91
  697.8 83.0 %all-reduce.20.cloned.1.call-done = f32[32,1024]{1,0:T(8,128)} async-done(((f32[32,1024]{1,0:T(8,128)}), f32[32,1024]{1,0:T(8,128)}) %all-reduce.20.cloned.1.call-update) | async-done | bytes 131088 | tf_op jit(solution)/shard_map/while/body/eval_jaxpr/psum | solution.py:91
  788.5 83.3 %all-reduce.20.cloned.1.call-done = f32[32,1024]{1,0:T(8,128)} async-done(((f32[32,1024]{1,0:T(8,128)}), f32[32,1024]{1,0:T(8,128)}) %all-reduce.20.cloned.1.call-update) | async-done | bytes 131088 | tf_op jit(solution)/shard_map/while/body/eval_jaxpr/psum | solution.py:91
  879.4 83.0 %all-reduce.20.cloned.1.call-done = f32[32,1024]{1,0:T(8,128)} async-done(((f32[32,1024]{1,0:T(8,128)}), f32[32,1024]{1,0:T(8,128)}) %all-reduce.20.cloned.1.call-update) | async-done | bytes 131088 | tf_op jit(solution)/shard_map/while/body/eval_jaxpr/psum | solution.py:91
  997.4 85.5 %all-reduce.12.cloned.1.call-done = bf16[128,2048]{1,0:T(8,128)(2,1)} async-done(((bf16[128,2048]{1,0:T(8,128)(2,1)}), bf16[128,2048]{1,0:T(8,128)(2,1)}) %all-reduce.12.cloned.1.call-update) | async-done | bytes 524304 | tf_op jit(solution)/shard_map/psum | solution.py:123
  1113.0 30.7 %reduce-scatter.3.cloned.1.call-done = f32[512,256]{1,0:T(8,128)} async-done(((f32[2048,256]{1,0:T(8,128)}), f32[512,256]{1,0:T(8,128)}) %reduce-scatter.3.cloned.1.call-update) | async-done | bytes 524304 | tf_op jit(solution)/shard_map/reduce_scatter | solution.py:130
  1145.4 64.8 %psum.83 = f32[]{:T(128)} all-reduce(f32[]{:T(128)} %multiply_reduce_fusion), channel_id=1, replica_groups=mesh['pipe'=2,'dp'=4,'tensor'=16] {'pipe','dp','tensor'}, use_global_device_ids=true, to_apply=%region_15.16 | all-reduce | flops 1 | bytes 8 | tf_op jit(solution)/shard_map/psum | solution.py:138
  1234.7 26.5 %all-reduce.16.cloned.1.call-done = bf16[256,256]{1,0:T(8,128)(2,1)} async-done(((bf16[256,256]{1,0:T(8,128)(2,1)}), bf16[256,256]{1,0:T(8,128)(2,1)}) %all-reduce.16.cloned.1.call-update) | async-done | bytes 131088 | tf_op jit(solution)/shard_map/psum | solution.py:144
  1263.9 30.7 %reduce-scatter.5.cloned.1.call-done = f32[512,256]{1,0:T(8,128)} async-done(((f32[2048,256]{1,0:T(8,128)}), f32[512,256]{1,0:T(8,128)}) %reduce-scatter.5.cloned.1.call-update) | async-done | bytes 524304 | tf_op jit(solution)/shard_map/reduce_scatter | solution.py:146
  (164 shorter events, 165.1 us)
Async XLA Ops:
  6.5 27.7 %all-gather.3.cloned.1.call-start = ((), (), s32[]{:S(2)}) async-start(), calls=%async_computation.2 | async-start | bytes 1310720 | tf_op jit(solution)/shard_map/all_gather | solution.py:30
  8.4 54.6 %all-reduce.8.cloned.1.call-start = ((), (), s32[]{:S(2)}) async-start(), calls=%async_computation.3 | async-start | bytes 131072 | tf_op jit(solution)/shard_map/psum | solution.py:32
  64.1 86.3 %all-reduce.18.cloned.1.call-start = ((), (), s32[]{:S(2)}) async-start(), calls=%async_computation.11 | async-start | bytes 262144 | tf_op jit(solution)/shard_map/while/body/eval_jaxpr/psum | solution.py:52
  156.1 84.0 %all-reduce.18.cloned.1.call-start = ((), (), s32[]{:S(2)}) async-start(), calls=%async_computation.11 | async-start | bytes 262144 | tf_op jit(solution)/shard_map/while/body/eval_jaxpr/psum | solution.py:52
  245.7 84.0 %all-reduce.18.cloned.1.call-start = ((), (), s32[]{:S(2)}) async-start(), calls=%async_computation.11 | async-start | bytes 262144 | tf_op jit(solution)/shard_map/while/body/eval_jaxpr/psum | solution.py:52
  335.3 84.0 %all-reduce.18.cloned.1.call-start = ((), (), s32[]{:S(2)}) async-start(), calls=%async_computation.11 | async-start | bytes 262144 | tf_op jit(solution)/shard_map/while/body/eval_jaxpr/psum | solution.py:52
  424.9 84.3 %all-reduce.18.cloned.1.call-start = ((), (), s32[]{:S(2)}) async-start(), calls=%async_computation.11 | async-start | bytes 262144 | tf_op jit(solution)/shard_map/while/body/eval_jaxpr/psum | solution.py:52
  514.9 84.3 %all-reduce.20.cloned.1.call-start = ((), (), s32[]{:S(2)}) async-start(), calls=%async_computation.12 | async-start | bytes 262144 | tf_op jit(solution)/shard_map/while/body/eval_jaxpr/psum | solution.py:91
  600.6 5.3 collective-permute-start.1
  605.9 84.3 %all-reduce.20.cloned.1.call-start = ((), (), s32[]{:S(2)}) async-start(), calls=%async_computation.12 | async-start | bytes 262144 | tf_op jit(solution)/shard_map/while/body/eval_jaxpr/psum | solution.py:91
  691.6 5.3 collective-permute-start.1
  696.8 84.0 %all-reduce.20.cloned.1.call-start = ((), (), s32[]{:S(2)}) async-start(), calls=%async_computation.12 | async-start | bytes 262144 | tf_op jit(solution)/shard_map/while/body/eval_jaxpr/psum | solution.py:91
  782.2 5.3 collective-permute-start.1
  787.5 84.3 %all-reduce.20.cloned.1.call-start = ((), (), s32[]{:S(2)}) async-start(), calls=%async_computation.12 | async-start | bytes 262144 | tf_op jit(solution)/shard_map/while/body/eval_jaxpr/psum | solution.py:91
  873.2 5.3 collective-permute-start.1
  878.5 84.0 %all-reduce.20.cloned.1.call-start = ((), (), s32[]{:S(2)}) async-start(), calls=%async_computation.12 | async-start | bytes 262144 | tf_op jit(solution)/shard_map/while/body/eval_jaxpr/psum | solution.py:91
  963.9 5.3 collective-permute-start.1
  969.1 25.9 %all-reduce.10.cloned.1.call-start = ((), (), s32[]{:S(2)}) async-start(), calls=%async_computation.4 | async-start | bytes 131072 | tf_op jit(solution)/shard_map/psum | solution.py:20
  969.9 113.0 %all-reduce.12.cloned.1.call-start = ((), (), s32[]{:S(2)}) async-start(), calls=%async_computation.5 | async-start | bytes 1048576 | tf_op jit(solution)/shard_map/psum | solution.py:123
  997.2 113.1 %all-reduce.14.cloned.1.call-start = ((), (), s32[]{:S(2)}) async-start(), calls=%async_computation.6 | async-start | bytes 131072 | tf_op jit(solution)/shard_map/psum | solution.py:125
  1085.1 58.6 %reduce-scatter.3.cloned.1.call-start = ((), (), s32[]{:S(2)}) async-start(), calls=%async_computation.7 | async-start | bytes 2621440 | tf_op jit(solution)/shard_map/reduce_scatter | solution.py:130
  1112.9 119.3 %all-gather.5.cloned.1.call-start = ((), (), s32[]{:S(2)}) async-start(), calls=%async_computation.8 | async-start | bytes 1310720 | tf_op jit(solution)/shard_map/all_gather | solution.py:142
  1212.9 48.3 %all-reduce.16.cloned.1.call-start = ((), (), s32[]{:S(2)}) async-start(), calls=%async_computation.9 | async-start | bytes 262144 | tf_op jit(solution)/shard_map/psum | solution.py:144
  1234.6 60.0 %reduce-scatter.5.cloned.1.call-start = ((), (), s32[]{:S(2)}) async-start(), calls=%async_computation.10 | async-start | bytes 2621440 | tf_op jit(solution)/shard_map/reduce_scatter | solution.py:146
  (14 other events, 1372.3 us)
Sparse Core Ops, SparseCore 0:
  9.0 25.1 all-gather.2
  36.8 26.1 all-reduce.7
  68.1 82.2 all-reduce.17
  159.8 80.2 all-reduce.17
  249.4 80.2 all-reduce.17
  339.0 80.2 all-reduce.17
  428.9 80.2 all-reduce.17
  518.9 80.2 all-reduce.19
  609.8 80.2 all-reduce.19
  700.5 80.2 all-reduce.19
  791.5 80.2 all-reduce.19
  882.1 80.2 all-reduce.19
  972.3 22.6 all-reduce.9
  998.1 84.6 all-reduce.11
  1085.2 25.0 all-reduce.13
  1113.1 30.5 reduce-scatter.2
  1213.0 19.2 all-gather.4
  1234.8 26.3 all-reduce.15
  1264.0 30.5 reduce-scatter.4
where the time goes:
time: 1300 us
  waiting for transfers between devices  986 us (76%)
  blocking collectives  222 us (17%)
  matrix products  29.6 us (2%)
  starting transfers between devices  29.1 us (2%)
  other arithmetic  20 us (2%)
  between operations  14.1 us (1%)
    psum x5, waiting for transfers between devices, backward_tick(): back_total = lax.psum(back_part, 'tensor')  416 us
    psum x5, waiting for transfers between devices, forward_tick(): summed, square_total = lax.psum((partial_value, squares), 'tensor')  260 us
    psum x5, blocking collectives, forward_tick(): summed, square_total = lax.psum((partial_value, squares), 'tensor')  157 us
    psum x1, waiting for transfers between devices, local(): embed_grad = lax.psum(value_part.astype(jnp.bfloat16), 'tensor')  85.5 us
    psum x1, blocking collectives, local(): lax.psum(jnp.sum(step_one * step_one), ('pipe', 'dp', 'tensor'))  64.8 us
    reduce_scatter x1, waiting for transfers between devices, local(): lax.psum_scatter(lax.dot_general(partial_value, second_dirs, (((0,), (0,)...  30.7 us
    reduce_scatter x1, waiting for transfers between devices, local(): lax.psum_scatter(lax.dot_general(partial_value, first_dirs, (((0,), (0,))...  30.7 us
    ppermute x10, starting transfers between devices, from_behind(): return lax.ppermute(shard, axis, pairs)  28.6 us
  transfers between devices with their start and end apart: 29, of which 29 were waited for; matrix products, arithmetic and copies ran while one was open for 1% of the time, Pallas kernels for 0%

commit v1 on v0

--- a/solution.py
+++ b/solution.py
@@ -88,7 +88,7 @@
         back_part = lax.dot_general(
             incoming, weight_out, (((1,), (1,)), ((), ())), preferred_element_type=jnp.float32
         )
-        back_total = lax.psum(back_part, "tensor")
+        back_total = jnp.sum(lax.all_gather(back_part, "tensor"), axis=0)
         gated_rows = inv_rms * summed
         inside = (gated_rows >= lowest) & (gated_rows <= highest)
         scaled_grad = (inv_rms * jnp.where(inside, back_total, 0.0)).astype(jnp.bfloat16)

time: 1300 us -> 1110 us (0.85)
  waiting for transfers between devices: 986 us -> 791 us
    psum x5 -> x0, waiting for transfers between devices: 416 us -> none  [backward_tick(): back_total = lax.psum(back_part, 'tensor')]
    all_gather x0 -> x5, waiting for transfers between devices: none -> 221 us  [backward_tick(): back_total = jnp.sum(lax.all_gather(back_part, 'tensor'), axis=0)]
where the time goes in v1:
time: 1110 us
  waiting for transfers between devices  791 us (71%)
  blocking collectives  222 us (20%)
  matrix products  29.6 us (3%)
  starting transfers between devices  27.5 us (2%)
  other arithmetic  24.1 us (2%)
  between operations  14.1 us (1%)
    psum x5, waiting for transfers between devices, forward_tick(): summed, square_total = lax.psum((partial_value, squares), 'tensor')  260 us
    all_gather x5, waiting for transfers between devices, backward_tick(): back_total = jnp.sum(lax.all_gather(back_part, 'tensor'), axis=0)  221 us
    psum x5, blocking collectives, forward_tick(): summed, square_total = lax.psum((partial_value, squares), 'tensor')  157 us
    psum x1, waiting for transfers between devices, local(): embed_grad = lax.psum(value_part.astype(jnp.bfloat16), 'tensor')  85.5 us
    psum x1, blocking collectives, local(): lax.psum(jnp.sum(step_one * step_one), ('pipe', 'dp', 'tensor'))  64.8 us
    reduce_scatter x1, waiting for transfers between devices, local(): lax.psum_scatter(lax.dot_general(partial_value, second_dirs, (((0,), (0,)...  30.7 us
    reduce_scatter x1, waiting for transfers between devices, local(): lax.psum_scatter(lax.dot_general(partial_value, first_dirs, (((0,), (0,))...  30.7 us
    ppermute x10, starting transfers between devices, from_behind(): return lax.ppermute(shard, axis, pairs)  27.1 us
  transfers between devices with their start and end apart: 29, of which 29 were waited for; matrix products, arithmetic and copies ran while one was open for 1% of the time, Pallas kernels for 0%

profile of v1, /device:TPU:1, one launch (start us, length us, event | category | flops | bytes accessed | tf_op | source)
XLA Modules:
  0.0 1110.9 jit_solution(2361168285941676303)
XLA Ops:
  8.5 25.7 %all-gather.7.cloned.1.call-done = bf16[2048,256]{1,0:T(8,128)(2,1)} async-done(((bf16[512,256]{1,0:T(8,128)(2,1)}), bf16[2048,256]{1,0:T(8,128)(2,1)}) %all-gather.7.cloned.1.call-update) | async-done | bytes 1048592 | tf_op jit(solution)/shard_map/all_gather | solution.py:30
  36.8 26.2 %all-reduce.7.cloned.1.call-done = bf16[128,256]{0,1:T(8,128)(2,1)} async-done(((bf16[128,256]{0,1:T(8,128)(2,1)}), bf16[128,256]{0,1:T(8,128)(2,1)}) %all-reduce.7.cloned.1.call-update) | async-done | bytes 65552 | tf_op jit(solution)/shard_map/psum | solution.py:32
  64.1 450.8 %while.37 = (s32[]{:T(128)}, bf16[32,256]{1,0:T(8,128)(2,1)S(1)}, bf16[4,32,256]{2,1,0:T(8,128)(2,1)S(1)}, f32[4,32,1024]{2,1,0:T(8,128)S(1)}, f32[4,32,1]{1,2,0...) while((s32[]{:T(128)}, bf16[32,256]{1,0:T(8,128)(2,1)S(1)}, ...), condition=%wide.region_5.6_spmd, body=%wide.region_1.5_spmd.sunk | while | flops 33882280 | bytes 2710062 | solution.py:75
  65.2 33.6 %psum.75 = f32[32]{0:T(128)S(1)} all-reduce(f32[32]{0:T(128)S(1)} %fusion.65), channel_id=1, replica_groups=mesh['pipe'=2,'dp'=4,'tensor'=16] {'tensor'}, use_global_device_ids=true, to_apply=%region_3.3 | all-reduce | flops 32 | bytes 256 | tf_op jit(solution)/shard_map/while/body/eval_jaxpr/psum | solution.py:52
  98.8 51.7 %all-reduce.17.cloned.1.call-done = f32[32,1024]{1,0:T(8,128)} async-done(((f32[32,1024]{1,0:T(8,128)}), f32[32,1024]{1,0:T(8,128)}) %all-reduce.17.cloned.1.call-update) | async-done | bytes 131088 | tf_op jit(solution)/shard_map/while/body/eval_jaxpr/psum | solution.py:52
  157.1 30.9 %psum.75 = f32[32]{0:T(128)S(1)} all-reduce(f32[32]{0:T(128)S(1)} %fusion.65), channel_id=1, replica_groups=mesh['pipe'=2,'dp'=4,'tensor'=16] {'tensor'}, use_global_device_ids=true, to_apply=%region_3.3 | all-reduce | flops 32 | bytes 256 | tf_op jit(solution)/shard_map/while/body/eval_jaxpr/psum | solution.py:52
  188.0 52.1 %all-reduce.17.cloned.1.call-done = f32[32,1024]{1,0:T(8,128)} async-done(((f32[32,1024]{1,0:T(8,128)}), f32[32,1024]{1,0:T(8,128)}) %all-reduce.17.cloned.1.call-update) | async-done | bytes 131088 | tf_op jit(solution)/shard_map/while/body/eval_jaxpr/psum | solution.py:52
  246.7 30.9 %psum.75 = f32[32]{0:T(128)S(1)} all-reduce(f32[32]{0:T(128)S(1)} %fusion.65), channel_id=1, replica_groups=mesh['pipe'=2,'dp'=4,'tensor'=16] {'tensor'}, use_global_device_ids=true, to_apply=%region_3.3 | all-reduce | flops 32 | bytes 256 | tf_op jit(solution)/shard_map/while/body/eval_jaxpr/psum | solution.py:52
  277.6 52.1 %all-reduce.17.cloned.1.call-done = f32[32,1024]{1,0:T(8,128)} async-done(((f32[32,1024]{1,0:T(8,128)}), f32[32,1024]{1,0:T(8,128)}) %all-reduce.17.cloned.1.call-update) | async-done | bytes 131088 | tf_op jit(solution)/shard_map/while/body/eval_jaxpr/psum | solution.py:52
  336.3 30.9 %psum.75 = f32[32]{0:T(128)S(1)} all-reduce(f32[32]{0:T(128)S(1)} %fusion.65), channel_id=1, replica_groups=mesh['pipe'=2,'dp'=4,'tensor'=16] {'tensor'}, use_global_device_ids=true, to_apply=%region_3.3 | all-reduce | flops 32 | bytes 256 | tf_op jit(solution)/shard_map/while/body/eval_jaxpr/psum | solution.py:52
  367.2 52.1 %all-reduce.17.cloned.1.call-done = f32[32,1024]{1,0:T(8,128)} async-done(((f32[32,1024]{1,0:T(8,128)}), f32[32,1024]{1,0:T(8,128)}) %all-reduce.17.cloned.1.call-update) | async-done | bytes 131088 | tf_op jit(solution)/shard_map/while/body/eval_jaxpr/psum | solution.py:52
  426.0 30.9 %psum.75 = f32[32]{0:T(128)S(1)} all-reduce(f32[32]{0:T(128)S(1)} %fusion.65), channel_id=1, replica_groups=mesh['pipe'=2,'dp'=4,'tensor'=16] {'tensor'}, use_global_device_ids=true, to_apply=%region_3.3 | all-reduce | flops 32 | bytes 256 | tf_op jit(solution)/shard_map/while/body/eval_jaxpr/psum | solution.py:52
  456.9 52.4 %all-reduce.17.cloned.1.call-done = f32[32,1024]{1,0:T(8,128)} async-done(((f32[32,1024]{1,0:T(8,128)}), f32[32,1024]{1,0:T(8,128)}) %all-reduce.17.cloned.1.call-update) | async-done | bytes 131088 | tf_op jit(solution)/shard_map/while/body/eval_jaxpr/psum | solution.py:52
  514.9 262.2 %while.38 = (s32[]{:T(128)}, bf16[32,256]{1,0:T(8,128)(2,1)S(1)}, bf16[4,32,256]{2,1,0:T(8,128)(2,1)S(1)}, pred[]{:T(512)}, s32[]{:T(128)}, /*index=5*/bf16[4,32...) while((s32[]{:T(128)}, bf16[32,256]{1,0:T(8,128)(2,1)S(1)}, ...), condition=%wide.region_9.10_spmd, body=%wide.region_6.9_spmd.sunk | while | flops 34447432 | bytes 10692308 | solution.py:117
  515.9 44.4 %all-gather.11.cloned.1.call-done = f32[512,1024]{1,0:T(8,128)} async-done(((f32[32,1024]{1,0:T(8,128)}), f32[512,1024]{1,0:T(8,128)}) %all-gather.11.cloned.1.call-update) | async-done | bytes 2097168 | tf_op jit(solution)/shard_map/while/body/eval_jaxpr/all_gather | solution.py:91
  568.4 44.4 %all-gather.11.cloned.1.call-done = f32[512,1024]{1,0:T(8,128)} async-done(((f32[32,1024]{1,0:T(8,128)}), f32[512,1024]{1,0:T(8,128)}) %all-gather.11.cloned.1.call-update) | async-done | bytes 2097168 | tf_op jit(solution)/shard_map/while/body/eval_jaxpr/all_gather | solution.py:91
  621.0 44.1 %all-gather.11.cloned.1.call-done = f32[512,1024]{1,0:T(8,128)} async-done(((f32[32,1024]{1,0:T(8,128)}), f32[512,1024]{1,0:T(8,128)}) %all-gather.11.cloned.1.call-update) | async-done | bytes 2097168 | tf_op jit(solution)/shard_map/while/body/eval_jaxpr/all_gather | solution.py:91
  673.3 44.4 %all-gather.11.cloned.1.call-done = f32[512,1024]{1,0:T(8,128)} async-done(((f32[32,1024]{1,0:T(8,128)}), f32[512,1024]{1,0:T(8,128)}) %all-gather.11.cloned.1.call-update) | async-done | bytes 2097168 | tf_op jit(solution)/shard_map/while/body/eval_jaxpr/all_gather | solution.py:91
  725.8 44.1 %all-gather.11.cloned.1.call-done = f32[512,1024]{1,0:T(8,128)} async-done(((f32[32,1024]{1,0:T(8,128)}), f32[512,1024]{1,0:T(8,128)}) %all-gather.11.cloned.1.call-update) | async-done | bytes 2097168 | tf_op jit(solution)/shard_map/while/body/eval_jaxpr/all_gather | solution.py:91
  805.3 85.5 %all-reduce.11.cloned.1.call-done = bf16[128,2048]{1,0:T(8,128)(2,1)} async-done(((bf16[128,2048]{1,0:T(8,128)(2,1)}), bf16[128,2048]{1,0:T(8,128)(2,1)}) %all-reduce.11.cloned.1.call-update) | async-done | bytes 524304 | tf_op jit(solution)/shard_map/psum | solution.py:123
  920.9 30.7 %reduce-scatter.3.cloned.1.call-done = f32[512,256]{1,0:T(8,128)} async-done(((f32[2048,256]{1,0:T(8,128)}), f32[512,256]{1,0:T(8,128)}) %reduce-scatter.3.cloned.1.call-update) | async-done | bytes 524304 | tf_op jit(solution)/shard_map/reduce_scatter | solution.py:130
  953.3 64.8 %psum.70 = f32[]{:T(128)} all-reduce(f32[]{:T(128)} %multiply_reduce_fusion), channel_id=1, replica_groups=mesh['pipe'=2,'dp'=4,'tensor'=16] {'pipe','dp','tensor'}, use_global_device_ids=true, to_apply=%region_15.16 | all-reduce | flops 1 | bytes 8 | tf_op jit(solution)/shard_map/psum | solution.py:138
  1042.6 26.5 %all-reduce.15.cloned.1.call-done = bf16[256,256]{1,0:T(8,128)(2,1)} async-done(((bf16[256,256]{1,0:T(8,128)(2,1)}), bf16[256,256]{1,0:T(8,128)(2,1)}) %all-reduce.15.cloned.1.call-update) | async-done | bytes 131088 | tf_op jit(solution)/shard_map/psum | solution.py:144
  1071.8 30.7 %reduce-scatter.5.cloned.1.call-done = f32[512,256]{1,0:T(8,128)} async-done(((f32[2048,256]{1,0:T(8,128)}), f32[512,256]{1,0:T(8,128)}) %reduce-scatter.5.cloned.1.call-update) | async-done | bytes 524304 | tf_op jit(solution)/shard_map/reduce_scatter | solution.py:146
  (169 shorter events, 167.5 us)
Async XLA Ops:
  6.5 27.7 %all-gather.7.cloned.1.call-start = ((), (), s32[]{:S(2)}) async-start(), calls=%async_computation.2 | async-start | bytes 1310720 | tf_op jit(solution)/shard_map/all_gather | solution.py:30
  8.4 54.6 %all-reduce.7.cloned.1.call-start = ((), (), s32[]{:S(2)}) async-start(), calls=%async_computation.3 | async-start | bytes 131072 | tf_op jit(solution)/shard_map/psum | solution.py:32
  64.1 86.3 %all-reduce.17.cloned.1.call-start = ((), (), s32[]{:S(2)}) async-start(), calls=%async_computation.11 | async-start | bytes 262144 | tf_op jit(solution)/shard_map/while/body/eval_jaxpr/psum | solution.py:52
  156.1 84.0 %all-reduce.17.cloned.1.call-start = ((), (), s32[]{:S(2)}) async-start(), calls=%async_computation.11 | async-start | bytes 262144 | tf_op jit(solution)/shard_map/while/body/eval_jaxpr/psum | solution.py:52
  245.7 84.0 %all-reduce.17.cloned.1.call-start = ((), (), s32[]{:S(2)}) async-start(), calls=%async_computation.11 | async-start | bytes 262144 | tf_op jit(solution)/shard_map/while/body/eval_jaxpr/psum | solution.py:52
  335.3 84.0 %all-reduce.17.cloned.1.call-start = ((), (), s32[]{:S(2)}) async-start(), calls=%async_computation.11 | async-start | bytes 262144 | tf_op jit(solution)/shard_map/while/body/eval_jaxpr/psum | solution.py:52
  424.9 84.3 %all-reduce.17.cloned.1.call-start = ((), (), s32[]{:S(2)}) async-start(), calls=%async_computation.11 | async-start | bytes 262144 | tf_op jit(solution)/shard_map/while/body/eval_jaxpr/psum | solution.py:52
  514.9 45.4 %all-gather.11.cloned.1.call-start = ((), (), s32[]{:S(2)}) async-start(), calls=%async_computation.12 | async-start | bytes 2228224 | tf_op jit(solution)/shard_map/while/body/eval_jaxpr/all_gather | solution.py:91
  562.5 5.0 collective-permute-start.1
  567.5 45.4 %all-gather.11.cloned.1.call-start = ((), (), s32[]{:S(2)}) async-start(), calls=%async_computation.12 | async-start | bytes 2228224 | tf_op jit(solution)/shard_map/while/body/eval_jaxpr/all_gather | solution.py:91
  615.1 5.0 collective-permute-start.1
  620.0 45.1 %all-gather.11.cloned.1.call-start = ((), (), s32[]{:S(2)}) async-start(), calls=%async_computation.12 | async-start | bytes 2228224 | tf_op jit(solution)/shard_map/while/body/eval_jaxpr/all_gather | solution.py:91
  667.3 5.0 collective-permute-start.1
  672.3 45.4 %all-gather.11.cloned.1.call-start = ((), (), s32[]{:S(2)}) async-start(), calls=%async_computation.12 | async-start | bytes 2228224 | tf_op jit(solution)/shard_map/while/body/eval_jaxpr/all_gather | solution.py:91
  719.9 5.0 collective-permute-start.1
  724.8 45.1 %all-gather.11.cloned.1.call-start = ((), (), s32[]{:S(2)}) async-start(), calls=%async_computation.12 | async-start | bytes 2228224 | tf_op jit(solution)/shard_map/while/body/eval_jaxpr/all_gather | solution.py:91
  772.1 4.9 collective-permute-start.1
  777.1 25.8 %all-reduce.9.cloned.1.call-start = ((), (), s32[]{:S(2)}) async-start(), calls=%async_computation.4 | async-start | bytes 131072 | tf_op jit(solution)/shard_map/psum | solution.py:20
  777.8 112.9 %all-reduce.11.cloned.1.call-start = ((), (), s32[]{:S(2)}) async-start(), calls=%async_computation.5 | async-start | bytes 1048576 | tf_op jit(solution)/shard_map/psum | solution.py:123
  805.1 113.1 %all-reduce.13.cloned.1.call-start = ((), (), s32[]{:S(2)}) async-start(), calls=%async_computation.6 | async-start | bytes 131072 | tf_op jit(solution)/shard_map/psum | solution.py:125
  893.0 58.6 %reduce-scatter.3.cloned.1.call-start = ((), (), s32[]{:S(2)}) async-start(), calls=%async_computation.7 | async-start | bytes 2621440 | tf_op jit(solution)/shard_map/reduce_scatter | solution.py:130
  920.8 119.3 %all-gather.9.cloned.1.call-start = ((), (), s32[]{:S(2)}) async-start(), calls=%async_computation.8 | async-start | bytes 1310720 | tf_op jit(solution)/shard_map/all_gather | solution.py:142
  1020.8 48.3 %all-reduce.15.cloned.1.call-start = ((), (), s32[]{:S(2)}) async-start(), calls=%async_computation.9 | async-start | bytes 262144 | tf_op jit(solution)/shard_map/psum | solution.py:144
  1042.5 60.0 %reduce-scatter.5.cloned.1.call-start = ((), (), s32[]{:S(2)}) async-start(), calls=%async_computation.10 | async-start | bytes 2621440 | tf_op jit(solution)/shard_map/reduce_scatter | solution.py:146
  (14 other events, 1180.2 us)
Sparse Core Ops, SparseCore 0:
  9.0 25.1 all-gather.6
  36.8 26.1 all-reduce.6
  68.1 82.2 all-reduce.16
  159.8 80.2 all-reduce.16
  249.4 80.2 all-reduce.16
  339.0 80.2 all-reduce.16
  428.9 80.2 all-reduce.16
  517.9 42.3 all-gather.10
  570.4 42.3 all-gather.10
  622.7 42.3 all-gather.10
  675.2 42.3 all-gather.10
  727.5 42.3 all-gather.10
  780.3 22.6 all-reduce.8
  806.0 84.6 all-reduce.10
  893.1 25.0 all-reduce.12
  921.0 30.5 reduce-scatter.2
  1020.9 19.2 all-gather.8
  1042.6 26.3 all-reduce.14
  1071.9 30.5 reduce-scatter.4
